TPU v7x, 32 devices: a whole 2x2x4 slice. The times are simulated.
32 devices in a mesh: row: 8 (over z, core), col: 4 (over y, x).
Axes of the slice: x: 2, y: 2, z: 4, core: 2. Of those that a mesh axis runs over, the one named last changes fastest.
Arguments:
- gram: bfloat16 [32768, 32768], P('row', 'col'), may hold values from -1 to 5, as said below
- start_basis: bfloat16 [32768, 256], P(('row', 'col')), may hold values from -12 to 12
- slab: float32 [32768, 4096], P('row', 'col'), may hold values from -6 to 6
Outputs:
- core_scaled: float32 [32768, 256], P(('row', 'col'))
- next_unfolding: float32 [4096, 256], P(('row', 'col'))
Inputs may be any that keep to these rules, and one draw needn't show every extreme that they name: gram is symmetric: entry (i, j) equals entry (j, i).
All inputs are finite; a program needn't handle non-finite values.
Results may differ from a plain program's by a relative error of at most 0.003.
Values may be sent and summed in bfloat16 or wider, within the bound.
A program may use at most 192 MiB of HBM per device.

v0:
```python
import math
import jax
import jax.numpy as jnp
from jax import lax
from jax.sharding import PartitionSpec as P

N = 32768
NMODE = 16


def body(gram, start_basis, slab):
    col_count = lax.axis_size("col")
    highest = lax.Precision.HIGHEST
    contract_rows = (((0,), (0,)), ((), ()))
    own_rows = lax.all_gather(start_basis, "col", axis=0, tiled=True)
    first_image = lax.psum_scatter(
        lax.dot_general(gram, own_rows, contract_rows, preferred_element_type=jnp.float32),
        "row",
        scatter_dimension=0,
        tiled=True,
    ).astype(jnp.bfloat16)
    col_rows = lax.all_gather(first_image, "row", axis=0, tiled=True)
    second_image = lax.psum_scatter(
        jnp.dot(gram, col_rows, preferred_element_type=jnp.float32),
        "col",
        scatter_dimension=0,
        tiled=True,
    )
    own_gram = lax.dot_general(
        second_image,
        second_image,
        contract_rows,
        precision=highest,
        preferred_element_type=jnp.float32,
    )
    small_gram = lax.psum(own_gram, ("row", "col"))
    factor = jnp.linalg.cholesky(small_gram)
    basis_cols = jax.scipy.linalg.solve_triangular(factor, second_image.T, lower=True).T
    block_basis = lax.all_gather(basis_cols, "col", axis=0, tiled=True)
    own_proj = lax.psum_scatter(
        lax.dot_general(
            block_basis, slab, contract_rows, precision=highest, preferred_element_type=jnp.float32
        ),
        "row",
        scatter_dimension=0,
        tiled=True,
    )
    core_out = basis_cols * math.sqrt(N)
    mode_share = NMODE // col_count
    grouped = own_proj.reshape(own_proj.shape[0], mode_share, own_proj.shape[1] // mode_share)
    regrouped = lax.all_to_all(grouped, "col", split_axis=0, concat_axis=1, tiled=True)
    return (
        core_out,
        regrouped.reshape(regrouped.shape[0] * regrouped.shape[1], regrouped.shape[2]),
    )


def solution(mesh):
    in_specs = (P("row", "col"), P(("row", "col"), None), P("row", "col"))
    out_specs = (P(("row", "col"), None), P(("row", "col"), None))
    return jax.shard_map(body, mesh=mesh, in_specs=in_specs, out_specs=out_specs, check_vma=False)
```

profile of v0, /device:TPU:0, one launch (start us, length us, event | category | flops | bytes accessed | tf_op | source)
XLA Modules:
  0.0 614.0 jit_solution(10611750755675535246)
XLA Ops:
  7.2 0.0 all-gather.4.cloned.1.call-start
  7.2 0.7 all-gather.4.cloned.1.call-update
  7.9 0.0 reduce-scatter.4.cloned.1.call-start
  7.9 39.8 %all-gather.4.cloned.1.call-done = bf16[4096,256]{1,0:T(8,128)(2,1)} async-done(((bf16[1024,256]{1,0:T(8,128)(2,1)}), bf16[4096,256]{1,0:T(8,128)(2,1)}) %all-gather.4.cloned.1.call-update) | async-done | bytes 2097168 | tf_op jit(solution)/shard_map/all_gather | solution.py:15
  47.8 30.0 %fusion.9 = f32[8192,256]{1,0:T(8,128)} fusion(bf16[4096,8192]{1,0:T(8,128)(2,1)} %param.3, bf16[4096,256]{1,0:T(8,128)(2,1)} %all-gather.4.cloned.1.call-done), kind=kOutput, calls=%fused_computation.32 | convolution fusion | flops 17179869184 | bytes 77594624 | tf_op jit(solution)/shard_map/dot_general | solution.py:17
  77.7 0.0 reduce-scatter.4.cloned.1.call-update
  77.7 0.0 all-gather.6.cloned.1.call-start
  77.8 89.6 %reduce-scatter.4.cloned.1.call-done = f32[1024,256]{1,0:T(8,128)} async-done(((f32[8192,256]{1,0:T(8,128)}), f32[1024,256]{1,0:T(8,128)}) %reduce-scatter.4.cloned.1.call-update) | async-done | bytes 1048592 | tf_op jit(solution)/shard_map/reduce_scatter | solution.py:16
  167.4 2.1 convert_element_type.3
  169.5 0.0 all-gather.6.cloned.1.call-update
  169.5 0.0 reduce-scatter.6.cloned.1.call-start
  169.6 45.4 %all-gather.6.cloned.1.call-done = bf16[8192,256]{1,0:T(8,128)(2,1)} async-done(((bf16[1024,256]{1,0:T(8,128)(2,1)}), bf16[8192,256]{1,0:T(8,128)(2,1)}) %all-gather.6.cloned.1.call-update) | async-done | bytes 4194320 | tf_op jit(solution)/shard_map/all_gather | solution.py:22
  215.0 29.2 %convolution_bitcast_fusion = f32[4096,256]{0,1:T(8,128)} fusion(bf16[8192,256]{1,0:T(8,128)(2,1)} %all-gather.6.cloned.1.call-done, bf16[4096,8192]{1,0:T(8,128)(2,1)} %param.3), kind=kOutput, calls=%fused_computation.2 | convolution fusion | flops 17179869184 | bytes 75497472 | tf_op jit(solution)/shard_map/dot_general | solution.py:24
  244.2 0.0 reduce-scatter.6.cloned.1.call-update
  244.2 0.0 all-reduce.3.cloned.1.call-start
  244.3 51.5 %reduce-scatter.6.cloned.1.call-done = f32[1024,256]{0,1:T(8,128)} async-done(((f32[4096,256]{0,1:T(8,128)}), f32[1024,256]{0,1:T(8,128)}) %reduce-scatter.6.cloned.1.call-update) | async-done | bytes 1048592 | tf_op jit(solution)/shard_map/reduce_scatter | solution.py:23
  295.8 0.0 copy-start
  295.8 3.4 fusion.10
  299.1 0.0 all-reduce.3.cloned.1.call-update
  299.1 0.2 all-gather.8.cloned.1.call-start
  299.4 128.9 %all-reduce.3.cloned.1.call-done = f32[256,256]{0,1:T(8,128)} async-done(((f32[256,256]{0,1:T(8,128)}), f32[256,256]{0,1:T(8,128)}) %all-reduce.3.cloned.1.call-update) | async-done | bytes 262160 | tf_op jit(solution)/shard_map/psum | solution.py:36
  428.3 1.1 copy.6
  429.4 1.0 fusion.2
  430.4 11.7 %cholesky.50 = f32[128,128]{1,0:T(8,128)S(1)} custom-call(f32[128,128]{1,0:T(8,128)S(1)} %cholesky.118), custom_call_target="Cholesky" | custom-call | tf_op jit(solution)/shard_map/jit(cholesky)/cholesky | solution.py:37
  442.1 9.8 %custom-call.15 = f32[1,128,128]{1,2,0:T(8,128)S(1)} custom-call(f32[1,128,128]{2,1,0:T(8,128)S(1)} %get-tuple-element.25), custom_call_target="InvertDiagBlocksLowerTriangular" | custom-call | tf_op jit(solution)/shard_map/jit(cholesky)/cholesky | solution.py:37
  452.0 0.2 constant_dynamic-update-slice_fusion.1
  452.2 0.3 convolution_subtract_fusion.1
  452.4 11.7 %cholesky.105 = f32[128,128]{1,0:T(8,128)S(1)} custom-call(f32[128,128]{1,0:T(8,128)S(1)} %convolution_subtract_fusion.1), custom_call_target="Cholesky" | custom-call | tf_op jit(solution)/shard_map/jit(cholesky)/cholesky | solution.py:37
  464.2 0.7 compare_reduce_fusion
  466.3 0.1 triangular_solve.57
  466.4 4.3 while.1
  466.6 0.6 fusion.25
  467.1 1.4 bitcast_dynamic-update-slice_fusion.2
  468.6 0.6 fusion.25
  469.2 1.4 bitcast_dynamic-update-slice_fusion.2
  470.6 19.7 %custom-call.16 = f32[2,128,128]{1,2,0:T(8,128)S(1)} custom-call(f32[2,128,128]{2,1,0:T(8,128)S(1)} %get-tuple-element.9), custom_call_target="InvertDiagBlocksLowerTriangular" | custom-call | tf_op jit(solution)/shard_map/jit(_solve_triangular)/triangular_solve | solution.py:38
  490.3 0.0 copy-done
  490.3 0.6 fusion
  491.0 0.6 convolution_subtract_fusion
  491.6 0.6 fusion.4
  492.2 1.0 maximum_bitcast_fusion
  493.2 0.0 all-gather.8.cloned.1.call-update
  493.3 0.0 reduce-scatter.8.cloned.1.call-start
  493.3 51.7 %all-gather.8.cloned.1.call-done = f32[4096,256]{0,1:T(8,128)} async-done(((f32[1024,256]{0,1:T(8,128)}), f32[4096,256]{0,1:T(8,128)}) %all-gather.8.cloned.1.call-update) | async-done | bytes 4194320 | tf_op jit(solution)/shard_map/all_gather | solution.py:39
  545.1 18.3 %fusion.11 = f32[256,1024]{1,0:T(8,128)} fusion(f32[4096,256]{0,1:T(8,128)} %all-gather.8.cloned.1.call-done, f32[4096,1024]{1,0:T(8,128)} %param.5), kind=kOutput, calls=%fused_computation.34 | convolution fusion | flops 12884901888 | bytes 22020096 | tf_op jit(solution)/shard_map/dot_general | solution.py:41
  563.3 0.0 reduce-scatter.8.cloned.1.call-update
  563.3 32.8 %reduce-scatter.8.cloned.1.call-done = f32[32,1024]{1,0:T(8,128)} async-done(((f32[256,1024]{1,0:T(8,128)}), f32[32,1024]{1,0:T(8,128)}) %reduce-scatter.8.cloned.1.call-update) | async-done | bytes 131088 | tf_op jit(solution)/shard_map/reduce_scatter | solution.py:40
  596.1 1.6 reshape.30
  597.7 3.7 all-to-all-start
  601.4 0.1 broadcast_multiply_fusion
  601.5 1.3 copy.8
  602.9 3.6 all-to-all-done
  606.4 0.7 reshape.31
  (10 shorter events, 0.2 us)
Async XLA Ops:
  7.2 40.6 %all-gather.4.cloned.1.call-start = ((), (), s32[]{:S(2)}) async-start(), calls=%async_computation.4 | async-start | bytes 2621440 | tf_op jit(solution)/shard_map/all_gather | solution.py:15
  7.9 159.5 %reduce-scatter.4.cloned.1.call-start = ((), (), s32[]{:S(2)}) async-start(), calls=%async_computation.5 | async-start | bytes 9437184 | tf_op jit(solution)/shard_map/reduce_scatter | solution.py:16
  77.7 137.3 %all-gather.6.cloned.1.call-start = ((), (), s32[]{:S(2)}) async-start(), calls=%async_computation.6 | async-start | bytes 4718592 | tf_op jit(solution)/shard_map/all_gather | solution.py:22
  169.5 126.2 %reduce-scatter.6.cloned.1.call-start = ((), (), s32[]{:S(2)}) async-start(), calls=%async_computation.7 | async-start | bytes 5242880 | tf_op jit(solution)/shard_map/reduce_scatter | solution.py:23
  244.2 184.1 %all-reduce.3.cloned.1.call-start = ((), (), s32[]{:S(2)}) async-start(), calls=%async_computation.8 | async-start | bytes 524288 | tf_op jit(solution)/shard_map/psum | solution.py:36
  295.8 194.6 %copy-start = (f32[1024,256]{0,1:T(8,128)S(1)}, f32[1024,256]{0,1:T(8,128)}, u32[]{:S(2)}) copy-start(f32[1024,256]{0,1:T(8,128)} %reduce-scatter.6.cloned.1.call-done) | copy-start | bytes 3145732
  299.1 245.9 %all-gather.8.cloned.1.call-start = ((), (), s32[]{:S(2)}) async-start(), calls=%async_computation.9 | async-start | bytes 5242880 | tf_op jit(solution)/shard_map/all_gather | solution.py:39
  493.3 102.9 %reduce-scatter.8.cloned.1.call-start = ((), (), s32[]{:S(2)}) async-start(), calls=%async_computation.10 | async-start | bytes 1179648 | tf_op jit(solution)/shard_map/reduce_scatter | solution.py:40
  597.7 8.7 %all-to-all-start = ((f32[32,4,256]{2,1,0:T(4,128)}), f32[32,4,256]{2,1,0:T(4,128)S(1)}, u32[]{:S(2)}, u32[]{:S(2)}) async-start(f32[32,4,256]{2,1,0:T(4,128)} %reshape.30), calls=%async_computation.3 | async-start | bytes 262144 | tf_op jit(solution)/shard_map/all_to_all | solution.py:51
Sparse Core Ops, SparseCore 0:
  9.8 37.8 all-gather.3
  77.9 89.5 reduce-scatter.3
  169.6 45.3 all-gather.5
  244.3 51.3 reduce-scatter.5
  301.7 126.5 all-reduce.2
  493.4 51.6 all-gather.7
  563.5 32.6 reduce-scatter.7
where the time goes:
time: 614 us
  waiting for transfers between devices  444 us (72%)
  matrix products  83.1 us (14%)
  other arithmetic  58 us (9%)
  between operations  15.6 us (3%)
  local copies, waits for them, and re-layouts  8.87 us (1%)
    psum x1, waiting for transfers between devices, body(): small_gram = lax.psum(own_gram, ('row', 'col'))  129 us
    reduce_scatter x1, waiting for transfers between devices, body(): lax.psum_scatter(lax.dot_general(gram, own_rows, contract_rows, preferred...  89.6 us
    all_gather x1, waiting for transfers between devices, body(): block_basis = lax.all_gather(basis_cols, 'col', axis=0, tiled=True)  51.7 us
    reduce_scatter x1, waiting for transfers between devices, body(): lax.psum_scatter(jnp.dot(gram, col_rows, preferred_element_type=jnp.float...  51.5 us
    all_gather x1, waiting for transfers between devices, body(): col_rows = lax.all_gather(first_image, 'row', axis=0, tiled=True)  45.4 us
    all_gather x1, waiting for transfers between devices, body(): own_rows = lax.all_gather(start_basis, 'col', axis=0, tiled=True)  39.8 us
    another operation x6, other arithmetic, body(): factor = jnp.linalg.cholesky(small_gram)  34 us
    reduce_scatter x1, waiting for transfers between devices, body(): lax.psum_scatter(lax.dot_general(block_basis, slab, contract_rows, precis...  32.8 us
  transfers between devices with their start and end apart: 8, of which 8 were waited for; matrix products, arithmetic and copies ran while one was open for 0% of the time, Pallas kernels for 0%

commit v1 on v0

--- a/solution.py
+++ b/solution.py
@@ -33,7 +33,7 @@
         precision=highest,
         preferred_element_type=jnp.float32,
     )
-    small_gram = lax.psum(own_gram, ("row", "col"))
+    small_gram = jnp.sum(lax.all_gather(own_gram, ("row", "col")), axis=0)
     factor = jnp.linalg.cholesky(small_gram)
     basis_cols = jax.scipy.linalg.solve_triangular(factor, second_image.T, lower=True).T
     block_basis = lax.all_gather(basis_cols, "col", axis=0, tiled=True)

time: 614 us -> 564 us (0.919)
  waiting for transfers between devices: 444 us -> 392 us
    psum x1 -> x0, waiting for transfers between devices: 129 us -> none  [body(): small_gram = lax.psum(own_gram, ('row', 'col'))]
    all_gather x0 -> x1, waiting for transfers between devices: none -> 77 us  [body(): small_gram = jnp.sum(lax.all_gather(own_gram, ('row', 'col')), axis=0)]
where the time goes in v1:
time: 564 us
  waiting for transfers between devices  392 us (70%)
  matrix products  83.2 us (15%)
  other arithmetic  61 us (11%)
  between operations  15.6 us (3%)
  local copies, waits for them, and re-layouts  7.92 us (1%)
    reduce_scatter x1, waiting for transfers between devices, body(): lax.psum_scatter(lax.dot_general(gram, own_rows, contract_rows, preferred...  89.6 us
    all_gather x1, waiting for transfers between devices, body(): small_gram = jnp.sum(lax.all_gather(own_gram, ('row', 'col')), axis=0)  77 us
    reduce_scatter x1, waiting for transfers between devices, body(): lax.psum_scatter(jnp.dot(gram, col_rows, preferred_element_type=jnp.float...  51.5 us
    all_gather x1, waiting for transfers between devices, body(): block_basis = lax.all_gather(basis_cols, 'col', axis=0, tiled=True)  51.3 us
    all_gather x1, waiting for transfers between devices, body(): col_rows = lax.all_gather(first_image, 'row', axis=0, tiled=True)  45.4 us
    all_gather x1, waiting for transfers between devices, body(): own_rows = lax.all_gather(start_basis, 'col', axis=0, tiled=True)  39.8 us
    another operation x6, other arithmetic, body(): factor = jnp.linalg.cholesky(small_gram)  34 us
    reduce_scatter x1, waiting for transfers between devices, body(): lax.psum_scatter(lax.dot_general(block_basis, slab, contract_rows, precis...  32.8 us
  transfers between devices with their start and end apart: 8, of which 8 were waited for; matrix products, arithmetic and copies ran while one was open for 0% of the time, Pallas kernels for 0%

profile of v1, /device:TPU:0, one launch (start us, length us, event | category | flops | bytes accessed | tf_op | source)
XLA Modules:
  0.0 563.7 jit_solution(6558482097479738117)
XLA Ops:
  7.2 0.0 all-gather.6.cloned.1.call-start
  7.2 0.7 all-gather.6.cloned.1.call-update
  7.9 0.0 reduce-scatter.4.cloned.1.call-start
  7.9 39.8 %all-gather.6.cloned.1.call-done = bf16[4096,256]{1,0:T(8,128)(2,1)} async-done(((bf16[1024,256]{1,0:T(8,128)(2,1)}), bf16[4096,256]{1,0:T(8,128)(2,1)}) %all-gather.6.cloned.1.call-update) | async-done | bytes 2097168 | tf_op jit(solution)/shard_map/all_gather | solution.py:15
  47.8 30.0 %fusion.9 = f32[8192,256]{1,0:T(8,128)} fusion(bf16[4096,8192]{1,0:T(8,128)(2,1)} %param.3, bf16[4096,256]{1,0:T(8,128)(2,1)} %all-gather.6.cloned.1.call-done), kind=kOutput, calls=%fused_computation.32 | convolution fusion | flops 17179869184 | bytes 77594624 | tf_op jit(solution)/shard_map/dot_general | solution.py:17
  77.7 0.0 reduce-scatter.4.cloned.1.call-update
  77.7 0.0 all-gather.8.cloned.1.call-start
  77.8 89.6 %reduce-scatter.4.cloned.1.call-done = f32[1024,256]{1,0:T(8,128)} async-done(((f32[8192,256]{1,0:T(8,128)}), f32[1024,256]{1,0:T(8,128)}) %reduce-scatter.4.cloned.1.call-update) | async-done | bytes 1048592 | tf_op jit(solution)/shard_map/reduce_scatter | solution.py:16
  167.4 2.1 convert_element_type.3
  169.5 0.0 all-gather.8.cloned.1.call-update
  169.5 0.0 reduce-scatter.6.cloned.1.call-start
  169.6 45.4 %all-gather.8.cloned.1.call-done = bf16[8192,256]{1,0:T(8,128)(2,1)} async-done(((bf16[1024,256]{1,0:T(8,128)(2,1)}), bf16[8192,256]{1,0:T(8,128)(2,1)}) %all-gather.8.cloned.1.call-update) | async-done | bytes 4194320 | tf_op jit(solution)/shard_map/all_gather | solution.py:22
  215.0 29.2 %convolution_bitcast_fusion = f32[4096,256]{0,1:T(8,128)} fusion(bf16[8192,256]{1,0:T(8,128)(2,1)} %all-gather.8.cloned.1.call-done, bf16[4096,8192]{1,0:T(8,128)(2,1)} %param.3), kind=kOutput, calls=%fused_computation.2 | convolution fusion | flops 17179869184 | bytes 75497472 | tf_op jit(solution)/shard_map/dot_general | solution.py:24
  244.2 0.0 reduce-scatter.6.cloned.1.call-update
  244.2 0.0 all-gather.12.cloned.1.call-start
  244.3 51.5 %reduce-scatter.6.cloned.1.call-done = f32[1024,256]{0,1:T(8,128)} async-done(((f32[4096,256]{0,1:T(8,128)}), f32[1024,256]{0,1:T(8,128)}) %reduce-scatter.6.cloned.1.call-update) | async-done | bytes 1048592 | tf_op jit(solution)/shard_map/reduce_scatter | solution.py:23
  295.8 0.0 copy-start
  295.8 3.5 fusion.10
  299.3 0.0 all-gather.12.cloned.1.call-update
  299.3 0.2 all-gather.10.cloned.1.call-start
  299.5 77.0 %all-gather.12.cloned.1.call-done = f32[8192,256]{1,0:T(8,128)} async-done(((f32[256,256]{1,0:T(8,128)}), f32[8192,256]{1,0:T(8,128)}) %all-gather.12.cloned.1.call-update) | async-done | bytes 8388624 | tf_op jit(solution)/shard_map/all_gather | solution.py:36
  376.5 3.9 reduce_sum.9
  380.5 0.1 copy.8
  380.6 11.7 %cholesky.50 = f32[128,128]{1,0:T(8,128)S(1)} custom-call(f32[128,128]{1,0:T(8,128)S(1)} %cholesky.118), custom_call_target="Cholesky" | custom-call | tf_op jit(solution)/shard_map/jit(cholesky)/cholesky | solution.py:37
  392.4 9.8 %custom-call.15 = f32[1,128,128]{1,2,0:T(8,128)S(1)} custom-call(f32[1,128,128]{2,1,0:T(8,128)S(1)} %get-tuple-element.27), custom_call_target="InvertDiagBlocksLowerTriangular" | custom-call | tf_op jit(solution)/shard_map/jit(cholesky)/cholesky | solution.py:37
  402.2 0.2 constant_dynamic-update-slice_fusion.1
  402.4 0.3 convolution_subtract_fusion.1
  402.7 11.7 %cholesky.105 = f32[128,128]{1,0:T(8,128)S(1)} custom-call(f32[128,128]{1,0:T(8,128)S(1)} %convolution_subtract_fusion.1), custom_call_target="Cholesky" | custom-call | tf_op jit(solution)/shard_map/jit(cholesky)/cholesky | solution.py:37
  414.5 0.7 compare_reduce_fusion
  416.6 0.1 triangular_solve.57
  416.6 4.3 while.1
  416.8 0.6 fusion.25
  417.4 1.4 bitcast_dynamic-update-slice_fusion.2
  418.9 0.6 fusion.25
  419.5 1.4 bitcast_dynamic-update-slice_fusion.2
  420.9 19.7 %custom-call.16 = f32[2,128,128]{1,2,0:T(8,128)S(1)} custom-call(f32[2,128,128]{2,1,0:T(8,128)S(1)} %get-tuple-element.9), custom_call_target="InvertDiagBlocksLowerTriangular" | custom-call | tf_op jit(solution)/shard_map/jit(_solve_triangular)/triangular_solve | solution.py:38
  440.6 0.0 copy-done
  440.6 0.6 fusion
  441.3 0.6 convolution_subtract_fusion
  441.8 0.6 fusion.4
  442.5 1.0 maximum_bitcast_fusion
  443.5 0.0 all-gather.10.cloned.1.call-update
  443.5 0.0 reduce-scatter.8.cloned.1.call-start
  443.6 51.3 %all-gather.10.cloned.1.call-done = f32[4096,256]{0,1:T(8,128)} async-done(((f32[1024,256]{0,1:T(8,128)}), f32[4096,256]{0,1:T(8,128)}) %all-gather.10.cloned.1.call-update) | async-done | bytes 4194320 | tf_op jit(solution)/shard_map/all_gather | solution.py:39
  494.9 18.3 %fusion.11 = f32[256,1024]{1,0:T(8,128)} fusion(f32[4096,256]{0,1:T(8,128)} %all-gather.10.cloned.1.call-done, f32[4096,1024]{1,0:T(8,128)} %param.5), kind=kOutput, calls=%fused_computation.34 | convolution fusion | flops 12884901888 | bytes 22020096 | tf_op jit(solution)/shard_map/dot_general | solution.py:41
  513.2 0.0 reduce-scatter.8.cloned.1.call-update
  513.2 32.8 %reduce-scatter.8.cloned.1.call-done = f32[32,1024]{1,0:T(8,128)} async-done(((f32[256,1024]{1,0:T(8,128)}), f32[32,1024]{1,0:T(8,128)}) %reduce-scatter.8.cloned.1.call-update) | async-done | bytes 131088 | tf_op jit(solution)/shard_map/reduce_scatter | solution.py:40
  546.0 1.6 reshape.30
  547.6 3.6 all-to-all-start
  551.2 0.1 broadcast_multiply_fusion
  551.3 1.3 copy.10
  552.6 3.6 all-to-all-done
  556.2 0.7 reshape.31
  (11 shorter events, 0.2 us)
Async XLA Ops:
  7.2 40.6 %all-gather.6.cloned.1.call-start = ((), (), s32[]{:S(2)}) async-start(), calls=%async_computation.4 | async-start | bytes 2621440 | tf_op jit(solution)/shard_map/all_gather | solution.py:15
  7.9 159.5 %reduce-scatter.4.cloned.1.call-start = ((), (), s32[]{:S(2)}) async-start(), calls=%async_computation.5 | async-start | bytes 9437184 | tf_op jit(solution)/shard_map/reduce_scatter | solution.py:16
  77.7 137.3 %all-gather.8.cloned.1.call-start = ((), (), s32[]{:S(2)}) async-start(), calls=%async_computation.6 | async-start | bytes 4718592 | tf_op jit(solution)/shard_map/all_gather | solution.py:22
  169.5 126.2 %reduce-scatter.6.cloned.1.call-start = ((), (), s32[]{:S(2)}) async-start(), calls=%async_computation.7 | async-start | bytes 5242880 | tf_op jit(solution)/shard_map/reduce_scatter | solution.py:23
  244.2 132.3 %all-gather.12.cloned.1.call-start = ((), (), s32[]{:S(2)}) async-start(), calls=%async_computation.10 | async-start | bytes 8650752 | tf_op jit(solution)/shard_map/all_gather | solution.py:36
  295.8 144.8 %copy-start = (f32[1024,256]{0,1:T(8,128)S(1)}, f32[1024,256]{0,1:T(8,128)}, u32[]{:S(2)}) copy-start(f32[1024,256]{0,1:T(8,128)} %reduce-scatter.6.cloned.1.call-done) | copy-start | bytes 3145732
  299.3 195.6 %all-gather.10.cloned.1.call-start = ((), (), s32[]{:S(2)}) async-start(), calls=%async_computation.8 | async-start | bytes 5242880 | tf_op jit(solution)/shard_map/all_gather | solution.py:39
  443.5 102.4 %reduce-scatter.8.cloned.1.call-start = ((), (), s32[]{:S(2)}) async-start(), calls=%async_computation.9 | async-start | bytes 1179648 | tf_op jit(solution)/shard_map/reduce_scatter | solution.py:40
  547.6 8.6 %all-to-all-start = ((f32[32,4,256]{2,1,0:T(4,128)}), f32[32,4,256]{2,1,0:T(4,128)S(1)}, u32[]{:S(2)}, u32[]{:S(2)}) async-start(f32[32,4,256]{2,1,0:T(4,128)} %reshape.30), calls=%async_computation.3 | async-start | bytes 262144 | tf_op jit(solution)/shard_map/all_to_all | solution.py:51
Sparse Core Ops, SparseCore 0:
  9.8 37.8 all-gather.5
  77.9 89.5 reduce-scatter.3
  169.6 45.3 all-gather.7
  244.3 51.3 reduce-scatter.5
  299.4 77.0 all-gather.11
  443.7 51.1 all-gather.9
  513.3 32.6 reduce-scatter.7
